TPU v7x, 512 devices: a whole 4x8x8 slice. The times are simulated.
512 devices in a mesh: dp: 16 (over y, core), expert: 32 (over x, z).
Axes of the slice: x: 4, y: 8, z: 8, core: 2. Of those that a mesh axis runs over, the one named last changes fastest.
Arguments:
- tokens: bfloat16 [65536, 2048], P(('dp', 'expert')), may hold values from -6 to 6
- out_grad: bfloat16 [65536, 2048], P(('dp', 'expert')), may hold values from -6 to 6
- expert_ids: int32 [65536, 8], P(('dp', 'expert')), may hold values from 0 to 127, all different within a row; in each aligned block of 128 rows (0 to 127, 128 to 255, ...) at most 10 rows name the same one
- gates: bfloat16 [65536, 8], P(('dp', 'expert')), may hold values from 0.049804688 to 0.59765625
- expert_weights: bfloat16 [32, 3, 2048, 384], P('expert', None, 'dp'), may hold values from -0.125 to 0.125
Outputs:
- token_grads: bfloat16 [65536, 2048], P(('dp', 'expert'))
- weight_grads: float32 [32, 3, 2048, 384], P('expert', None, 'dp')
Inputs may be any that keep to these rules, and one draw needn't show every extreme that they name: `expert_ids`: each row names 8 different experts; among the 128 rows of one device no expert is named more than 10 times, a bound that some block reaches.
All inputs are finite; a program needn't handle non-finite values.
Results may differ from a plain program's by a relative error of at most 0.0065.
Values may be sent and summed in bfloat16 or wider, within the bound.
A program may use at most 64 MiB of HBM per device.

v0:
```python
import jax
import jax.numpy as jnp
from jax import lax
from jax.sharding import PartitionSpec as P

EXPERTS = 128
SLOTS = 10


def route_tables(expert_ids, gates, window):
    token_rows, top_count = expert_ids.shape
    flat_ids = expert_ids.reshape(token_rows * top_count)
    onehot = (flat_ids[:, None] == jnp.arange(EXPERTS, dtype=jnp.int32)[None, :]).astype(jnp.int32)
    before = jnp.cumsum(onehot, axis=0) - onehot
    slot_index = jnp.sum(before * onehot, axis=1)
    target = jnp.where(flat_ids < window, flat_ids * SLOTS + slot_index, -1)
    picked = (target[None, :] == jnp.arange(window * SLOTS, dtype=jnp.int32)[:, None]).astype(
        jnp.float32
    )
    picked = picked.reshape(window * SLOTS, token_rows, top_count)
    token_table = jnp.sum(picked, axis=2).astype(jnp.bfloat16)
    gate_table = jnp.sum(picked * gates.astype(jnp.float32)[None, :, :], axis=2).astype(
        jnp.bfloat16
    )
    return (token_table, gate_table)


def inner_rows(first_op, second_op):
    return lax.dot_general(
        first_op, second_op, (((0,), (0,)), ((), ())), preferred_element_type=jnp.float32
    )


def inner_cols(first_op, second_op):
    return lax.dot_general(
        first_op, second_op, (((1,), (1,)), ((), ())), preferred_element_type=jnp.float32
    )


def on_device(tokens, out_grad, expert_ids, gates, expert_weights):
    window = lax.axis_size("expert")
    groups = lax.axis_size("dp")
    model_width = tokens.shape[1]
    hidden_units = expert_weights.shape[3]
    owned_rows = model_width // groups
    token_table, gate_table = route_tables(expert_ids, gates, window)
    sent_rows = jnp.dot(token_table, tokens, preferred_element_type=jnp.float32).astype(
        jnp.bfloat16
    )
    sent_grads = jnp.dot(gate_table, out_grad, preferred_element_type=jnp.float32).astype(
        jnp.bfloat16
    )
    sent_rows = sent_rows.reshape(window, SLOTS, model_width)
    sent_grads = sent_grads.reshape(window, SLOTS, model_width)
    got_rows, got_grads = (
        lax.all_to_all(sent_rows, "expert", split_axis=0, concat_axis=0, tiled=True),
        lax.all_to_all(sent_grads, "expert", split_axis=0, concat_axis=0, tiled=True),
    )
    expert_rows = got_rows.reshape(window * SLOTS, model_width)
    expert_grads = got_grads.reshape(window * SLOTS, model_width)
    full_weights = lax.all_gather(expert_weights, "dp", axis=2, tiled=True)
    gate_act = jnp.dot(expert_rows, full_weights[0, 0], preferred_element_type=jnp.float32)
    up_act = jnp.dot(expert_rows, full_weights[0, 1], preferred_element_type=jnp.float32)
    w_gate = full_weights[0, 0]
    w_up = full_weights[0, 1]
    w_down = full_weights[0, 2]
    logistic = jax.nn.sigmoid(gate_act)
    swish_out = gate_act * logistic
    hidden = (swish_out * up_act).astype(jnp.bfloat16)
    grad_hidden = jnp.dot(expert_grads, w_down, preferred_element_type=jnp.float32)
    grad_up = (grad_hidden * swish_out).astype(jnp.bfloat16)
    grad_gate = (grad_hidden * up_act * logistic * (1.0 + gate_act * (1.0 - logistic))).astype(
        jnp.bfloat16
    )
    down_part = inner_rows(expert_grads, hidden).astype(jnp.bfloat16)
    expert_back = (inner_cols(grad_gate, w_gate) + inner_cols(grad_up, w_up)).astype(jnp.bfloat16)
    returned = lax.all_to_all(
        expert_back.reshape(window, SLOTS, model_width),
        "expert",
        split_axis=0,
        concat_axis=0,
        tiled=True,
    )
    token_grads = inner_rows(token_table, returned.reshape(window * SLOTS, model_width)).astype(
        jnp.bfloat16
    )
    gate_part = inner_rows(expert_rows, grad_gate).astype(jnp.bfloat16)
    up_part = inner_rows(expert_rows, grad_up).astype(jnp.bfloat16)
    pieces = jnp.stack([gate_part, up_part, down_part]).reshape(3, groups, owned_rows, hidden_units)
    received = lax.all_to_all(pieces, "dp", split_axis=1, concat_axis=1, tiled=True)
    weight_grads = jnp.sum(received.astype(jnp.float32), axis=1)
    return (token_grads, weight_grads[None])


def solution(mesh):
    return jax.shard_map(
        on_device,
        mesh=mesh,
        in_specs=(
            P(("dp", "expert"), None),
            P(("dp", "expert"), None),
            P(("dp", "expert"), None),
            P(("dp", "expert"), None),
            P("expert", None, "dp", None),
        ),
        out_specs=(P(("dp", "expert"), None), P("expert", None, "dp", None)),
        check_vma=False,
    )
```

profile of v0, /device:TPU:6, one launch (start us, length us, event | category | flops | bytes accessed | tf_op | source)
XLA Modules:
  0.0 321.9 jit_solution(10423859914206272215)
XLA Ops:
  7.2 0.7 all-gather.2.cloned.1.call-update
  7.9 0.8 copy.42
  8.9 0.7 convert_element_type.57
  10.6 1.0 select_reduce_fusion
  11.6 0.5 convolution_convert_fusion.3
  12.1 1.6 reshape.72
  13.8 13.6 %all-to-all-start.1 = ((bf16[32,10,2048]{2,1,0:T(8,128)(2,1)}), bf16[32,10,2048]{2,1,0:T(8,128)(2,1)S(1)}, u32[]{:S(2)}, u32[]{:S(2)}) async-start(bf16[32,10,2048]{2,1,0:T(8,128)(2,1)} %reshape.72), calls=%async_computation.1 | async-start | bytes 4194304 | tf_op jit(solution)/shard_map/all_to_all | solution.py:56
  27.4 1.6 convolution_convert_fusion.4
  28.9 3.4 %reshape.70 = bf16[32,10,2048]{2,1,0:T(8,128)(2,1)} reshape(bf16[320,2048]{1,0:T(8,128)(2,1)} %convolution_convert_fusion.4) | data formatting | bytes 2621440 | tf_op jit(solution)/shard_map/reshape | solution.py:54
  32.3 42.9 %all-to-all-done.1 = bf16[32,10,2048]{2,1,0:T(8,128)(2,1)S(1)} async-done(((bf16[32,10,2048]{2,1,0:T(8,128)(2,1)}), bf16[32,10,2048]{2,1,0:T(8,128)(2,1)S(1)}, u32[]{:S(2)}, u32[]{:S(2)}) %all-to-all-start.1) | async-done | bytes 1310752 | tf_op jit(solution)/shard_map/all_to_all | solution.py:56
  75.2 8.4 %all-to-all-start = ((bf16[32,10,2048]{2,1,0:T(8,128)(2,1)}), bf16[32,10,2048]{2,1,0:T(8,128)(2,1)}, u32[]{:S(2)}, u32[]{:S(2)}) async-start(bf16[32,10,2048]{2,1,0:T(8,128)(2,1)} %reshape.70), calls=%async_computation | async-start | bytes 4194304 | tf_op jit(solution)/shard_map/all_to_all | solution.py:57
  83.6 1.3 reshape.73
  84.9 46.3 %all-to-all-done = bf16[32,10,2048]{2,1,0:T(8,128)(2,1)} async-done(((bf16[32,10,2048]{2,1,0:T(8,128)(2,1)}), bf16[32,10,2048]{2,1,0:T(8,128)(2,1)}, u32[]{:S(2)}, u32[]{:S(2)}) %all-to-all-start) | async-done | bytes 1310752 | tf_op jit(solution)/shard_map/all_to_all | solution.py:57
  131.2 2.5 reshape.71
  133.8 2.7 fusion.4
  136.5 0.5 copy-done.1
  137.0 0.9 fusion.2
  137.9 0.9 multiply_convert_fusion.1
  138.9 0.9 fusion.3
  139.8 0.9 fusion
  140.7 1.6 reshape.74
  142.3 8.5 %all-to-all-start.2 = ((bf16[32,10,2048]{2,1,0:T(8,128)(2,1)}), bf16[32,10,2048]{2,1,0:T(8,128)(2,1)S(1)}, u32[]{:S(2)}, u32[]{:S(2)}) async-start(bf16[32,10,2048]{2,1,0:T(8,128)(2,1)} %reshape.74), calls=%async_computation.2 | async-start | bytes 4194304 | tf_op jit(solution)/shard_map/all_to_all | solution.py:77
  150.8 2.6 convolution_convert_fusion.1
  153.5 1.2 convolution_convert_fusion.2
  155.0 1.2 convolution_convert_fusion
  156.2 2.5 pad_maximum_fusion
  158.7 39.6 %all-to-all-done.2 = bf16[32,10,2048]{2,1,0:T(8,128)(2,1)S(1)} async-done(((bf16[32,10,2048]{2,1,0:T(8,128)(2,1)}), bf16[32,10,2048]{2,1,0:T(8,128)(2,1)S(1)}, u32[]{:S(2)}, u32[]{:S(2)}) %all-to-all-start.2) | async-done | bytes 1310752 | tf_op jit(solution)/shard_map/all_to_all | solution.py:77
  198.3 7.2 %all-to-all-start.3 = ((bf16[3,16,128,384]{3,2,0,1:T(8,128)(2,1)}), bf16[3,16,128,384]{3,2,0,1:T(8,128)(2,1)}, u32[]{:S(2)}, u32[]{:S(2)}) async-start(bf16[3,16,128,384]{3,2,0,1:T(8,128)(2,1)} %pad_maximum_fusion), calls=%async_computation.3 | async-start | bytes 9437184 | tf_op jit(solution)/shard_map/all_to_all | solution.py:90
  205.5 1.3 reshape.75
  206.9 2.6 convolution_convert_fusion.5
  209.4 101.6 %all-to-all-done.3 = bf16[3,16,128,384]{3,2,0,1:T(8,128)(2,1)} async-done(((bf16[3,16,128,384]{3,2,0,1:T(8,128)(2,1)}), bf16[3,16,128,384]{3,2,0,1:T(8,128)(2,1)}, u32[]{:S(2)}, u32[]{:S(2)}) %all-to-all-start.3) | async-done | bytes 4718624 | tf_op jit(solution)/shard_map/all_to_all | solution.py:90
  311.1 4.0 %convert_reduce_fusion = f32[3,128,384]{2,1,0:T(8,128)} fusion(bf16[3,16,128,384]{3,2,0,1:T(8,128)(2,1)} %all-to-all-done.3), kind=kLoop, calls=%fused_computation | loop fusion | flops 4571136 | bytes 5308416 | tf_op jit(solution)/shard_map/reduce_sum | solution.py:91
  (42 shorter events, 1.6 us)
Async XLA Ops:
  7.2 4.5 %copy-start = (bf16[128,2048]{1,0:T(8,128)(2,1)S(1)}, bf16[128,2048]{1,0:T(8,128)(2,1)}, u32[]{:S(2)}) copy-start(bf16[128,2048]{1,0:T(8,128)(2,1)} %param.5) | copy-start | bytes 1572868
  7.2 126.6 %all-gather.2.cloned.1.call-start = ((), (), s32[]{:S(2)}) async-start(), calls=%async_computation.4 | async-start | bytes 5013504 | tf_op jit(solution)/shard_map/all_gather | solution.py:61
  9.7 0.9 copy-start.9
  13.8 13.6 %copy-start.6 = (bf16[128,2048]{1,0:T(8,128)(2,1)S(1)}, bf16[128,2048]{1,0:T(8,128)(2,1)}, u32[]{:S(2)}) copy-start(bf16[128,2048]{1,0:T(8,128)(2,1)} %param.6) | copy-start | bytes 1572868
  13.8 61.4 %all-to-all-start.1 = ((bf16[32,10,2048]{2,1,0:T(8,128)(2,1)}), bf16[32,10,2048]{2,1,0:T(8,128)(2,1)S(1)}, u32[]{:S(2)}, u32[]{:S(2)}) async-start(bf16[32,10,2048]{2,1,0:T(8,128)(2,1)} %reshape.72), calls=%async_computation.1 | async-start | bytes 4194304 | tf_op jit(solution)/shard_map/all_to_all | solution.py:56
  75.2 56.0 %all-to-all-start = ((bf16[32,10,2048]{2,1,0:T(8,128)(2,1)}), bf16[32,10,2048]{2,1,0:T(8,128)(2,1)}, u32[]{:S(2)}, u32[]{:S(2)}) async-start(bf16[32,10,2048]{2,1,0:T(8,128)(2,1)} %reshape.70), calls=%async_computation | async-start | bytes 4194304 | tf_op jit(solution)/shard_map/all_to_all | solution.py:57
  84.9 48.8 %copy-start.2 = (bf16[320,2048]{1,0:T(8,128)(2,1)S(1)}, bf16[320,2048]{1,0:T(8,128)(2,1)}, u32[]{:S(2)}) copy-start(bf16[320,2048]{1,0:T(8,128)(2,1)} %reshape.73) | copy-start | bytes 3932164
  133.7 4.2 %copy-start.4 = (bf16[320,2048]{1,0:T(8,128)(2,1)}, bf16[320,2048]{1,0:T(8,128)(2,1)S(1)}, u32[]{:S(2)}) copy-start(bf16[320,2048]{1,0:T(8,128)(2,1)S(1)} %reshape.71) | copy-start | bytes 3932164
  133.8 3.3 %copy-start.1 = (bf16[1,3,2048,384]{3,2,1,0:T(8,128)(2,1)S(1)}, bf16[1,3,2048,384]{3,2,1,0:T(8,128)(2,1)}, u32[]{:S(2)}) copy-start(bf16[1,3,2048,384]{3,2,1,0:T(8,128)(2,1)} %all-gather.2.cloned.1.call-done) | copy-start | bytes 14155780
  137.0 0.9 copy-start.10
  137.9 1.0 copy-start.12
  138.9 0.9 copy-start.7
  142.3 8.5 %copy-start.8 = (bf16[320,384]{1,0:T(8,128)(2,1)S(1)}, bf16[320,384]{1,0:T(8,128)(2,1)}, u32[]{:S(2)}) copy-start(bf16[320,384]{1,0:T(8,128)(2,1)} %copy-done.7) | copy-start | bytes 737284
  142.3 56.0 %all-to-all-start.2 = ((bf16[32,10,2048]{2,1,0:T(8,128)(2,1)}), bf16[32,10,2048]{2,1,0:T(8,128)(2,1)S(1)}, u32[]{:S(2)}, u32[]{:S(2)}) async-start(bf16[32,10,2048]{2,1,0:T(8,128)(2,1)} %reshape.74), calls=%async_computation.2 | async-start | bytes 4194304 | tf_op jit(solution)/shard_map/all_to_all | solution.py:77
  150.8 2.6 copy-start.3
  153.5 1.3 copy-start.5
  153.5 1.4 copy-start.11
  153.5 1.6 copy-start.13
  198.3 112.8 %all-to-all-start.3 = ((bf16[3,16,128,384]{3,2,0,1:T(8,128)(2,1)}), bf16[3,16,128,384]{3,2,0,1:T(8,128)(2,1)}, u32[]{:S(2)}, u32[]{:S(2)}) async-start(bf16[3,16,128,384]{3,2,0,1:T(8,128)(2,1)} %pad_maximum_fusion), calls=%async_computation.3 | async-start | bytes 9437184 | tf_op jit(solution)/shard_map/all_to_all | solution.py:90
Sparse Core Ops, SparseCore 0:
  10.1 49.0 all-gather.1
where the time goes:
time: 325 us; the launch traced here: 322 us
  waiting for transfers between devices  231 us (71%)
  starting transfers between devices  37.8 us (12%)
  matrix products  15.9 us (5%)
  between operations  14.4 us (4%)
  local copies, waits for them, and re-layouts  14 us (4%)
  other arithmetic  8.77 us (3%)
    all_to_all x1, waiting for transfers between devices, on_device(): lax.all_to_all(pieces, 'dp', split_axis=1, concat_axis=1, tiled=True)  102 us
    all_to_all x1, waiting for transfers between devices, on_device(): lax.all_to_all(sent_grads, 'expert', split_axis=0, concat_axis=0, tiled=T...  46.3 us
    all_to_all x1, waiting for transfers between devices, on_device(): lax.all_to_all(sent_rows, 'expert', split_axis=0, concat_axis=0, tiled=True)  42.9 us
    all_to_all x1, waiting for transfers between devices, on_device(): lax.all_to_all(expert_back.reshape(window, SLOTS, model_width), 'expert',...  39.6 us
    all_to_all x1, starting transfers between devices, on_device(): lax.all_to_all(sent_rows, 'expert', split_axis=0, concat_axis=0, tiled=True)  13.6 us
    all_to_all x1, starting transfers between devices, on_device(): lax.all_to_all(expert_back.reshape(window, SLOTS, model_width), 'expert',...  8.51 us
    all_to_all x1, starting transfers between devices, on_device(): lax.all_to_all(sent_grads, 'expert', split_axis=0, concat_axis=0, tiled=T...  8.43 us
    dot_general x4, matrix products, inner_rows(): lax.dot_general(first_op, second_op, (((0,), (0,)), ((), ())), preferred_...  7.57 us
  transfers between devices with their start and end apart: 5, of which 4 were waited for; matrix products, arithmetic and copies ran while one was open for 8% of the time, Pallas kernels for 0%

commit v1 on v0

v1 whole, which is shorter than its diff:
```python
import jax
import jax.numpy as jnp
from jax import lax
from jax.experimental import pallas as pl
from jax.experimental.pallas import tpu as pltpu
from jax.sharding import PartitionSpec as P

MESH = pl.DeviceIdType.MESH
NX, NZ, NY = 4, 8, 8
PEERS = NX * NZ
TOK, D, FF = 128, 2048, 384
HALF = D // 2
F32, BF16 = jnp.float32, jnp.bfloat16


def mm(a, b, ca, cb):
    return lax.dot_general(a, b, (((ca,), (cb,)), ((), ())), preferred_element_type=F32)


def kernel(
    tok_ref, og_ref, ids_ref, gates_ref, w_ref,
    tg_ref, wg_ref,
    both, sa, sb, ra, rb, w, z, ba, bb, ca, cb, own, pxs, pxr, rss, rsr, tl, tr,
    load_sem, sa_s, sa_r, sb_s, sb_r, ba_s, ba_r, bb_s, bb_r,
    ring_s, ring_r, par_s, par_r, px_s, px_r, rs_s, rs_r,
):
    e_me = lax.axis_index("expert")
    g_me = lax.axis_index("dp")
    mx, mz = e_me // NZ, e_me % NZ
    my, mc = g_me // 2, g_me % 2
    other = 1 - mc
    partner = my * 2 + other

    def ahead(slot):
        return ((mx + slot // NZ) % NX) * NZ + (mz + slot % NZ) % NZ

    def behind(slot):
        return ((mx + NX - slot // NZ) % NX) * NZ + (mz + NZ - slot % NZ) % NZ

    def along(step):
        return ((my + NY + step) % NY) * 2 + mc

    def remote(src, dst, ss, rs, **where):
        return pltpu.make_async_remote_copy(
            src_ref=src, dst_ref=dst, send_sem=ss, recv_sem=rs, device_id=where, device_id_type=MESH
        )

    def disp_a(slot):
        return remote(sa.at[slot], ra.at[slot], sa_s.at[slot], sa_r.at[slot], expert=ahead(slot))

    def disp_b(slot):
        return remote(sb.at[slot], rb.at[slot], sb_s.at[slot], sb_r.at[slot], expert=ahead(slot))

    def ret_a(slot):
        return remote(ba.at[slot], ca.at[slot], ba_s.at[slot], ba_r.at[slot], expert=behind(slot))

    def ret_b(slot):
        return remote(bb.at[slot], cb.at[slot], bb_s.at[slot], bb_r.at[slot], expert=behind(slot))

    def loop(lo, hi, act):
        lax.fori_loop(lo, hi, lambda i, carry: (act(i), carry)[1], 0)

    def shard(g):
        return w.at[:, pl.ds(pl.multiple_of(g * 128, 128), 128), :]

    def ring(lane, dist):
        step = 1 - 2 * lane
        g = along(-step * dist)
        src = w_ref if dist == 0 else shard(g)
        return remote(src, shard(g), ring_s.at[lane, dist], ring_r.at[lane, dist], dp=along(step))

    def ring_in(lane, dist):
        step = 1 - 2 * lane
        g = along(-step * dist)
        return remote(
            w_ref, shard(g), ring_s.at[lane, dist - 1], ring_r.at[lane, dist - 1], dp=along(step)
        )

    def share(rel):
        g = along(rel)
        src = w_ref if rel == 0 else shard(g)
        return remote(src, shard(g), par_s.at[rel + 4], par_r.at[rel + 4], dp=partner)

    def share_in(rel):
        g = ((my + NY + rel) % NY) * 2 + other
        return remote(w_ref, shard(g), par_s.at[rel + 4], par_r.at[rel + 4], dp=partner)

    loads = [
        pltpu.make_async_copy(tok_ref, both.at[pl.ds(0, TOK)], load_sem.at[0]),
        pltpu.make_async_copy(og_ref, both.at[pl.ds(TOK, TOK)], load_sem.at[1]),
    ]
    for c in loads:
        c.start()

    barrier = pltpu.get_barrier_semaphore()

    def greet(slot):
        pl.semaphore_signal(barrier, inc=1, device_id={"expert": ahead(slot)}, device_id_type=MESH)

    loop(1, PEERS, greet)
    for g in (along(1), along(-1), partner):
        pl.semaphore_signal(barrier, inc=1, device_id={"dp": g}, device_id_type=MESH)

    lane = lax.broadcasted_iota(jnp.int32, (TOK, 128), 1)
    row = lax.broadcasted_iota(jnp.int32, (TOK, 128), 0)
    ids = ids_ref[...]
    gates = gates_ref[...].astype(F32)
    named = jnp.zeros((TOK, 128), F32)
    gate_of = jnp.zeros((TOK, 128), F32)
    for k in range(8):
        hit = ids[:, k : k + 1] == lane
        named = named + jnp.where(hit, 1.0, 0.0)
        gate_of = gate_of + jnp.where(hit, gates[:, k : k + 1], 0.0)
    earlier = jnp.where(lane < row, 1.0, 0.0).astype(BF16)
    before = mm(earlier, named.astype(BF16), 1, 0)
    slots = jnp.where(named > 0.5, before, -1.0).astype(BF16)
    gate_of = gate_of.astype(BF16)

    def place(at, chunk):
        dest = ((mx + chunk) % NX) * NZ + ((mz + (at >> 4)) & (NZ - 1))
        return dest, (at & 7).astype(F32), (at & 15) >= 8

    def place_rest(at):
        block = at >> 2
        dest = ((mx + (block >> 3)) & (NX - 1)) * NZ + ((mz + (block & 7)) & (NZ - 1))
        return dest, (8 + (at & 1)).astype(F32), (at & 3) >= 2

    def table(dest, wanted, upper):
        pick = jnp.where(lane == dest, 1.0, 0.0).astype(BF16)
        hit = mm(pick, slots, 1, 1) == wanted
        gate = mm(pick, gate_of, 1, 1)
        first = jnp.where(hit & jnp.logical_not(upper), 1.0, 0.0).astype(BF16)
        second = jnp.where(hit & upper, gate, 0.0).astype(BF16)
        return jnp.concatenate([first, second], axis=1)

    def table_back(chunk, dest, wanted, upper):
        pick = jnp.where(row == dest, 1.0, 0.0).astype(BF16)
        hit = mm(slots, pick, 1, 0) == wanted
        tl[:, pl.ds(128 * chunk, 128)] = jnp.where(hit & jnp.logical_not(upper), 1.0, 0.0).astype(BF16)
        tr[:, pl.ds(128 * chunk, 128)] = jnp.where(hit & upper, 1.0, 0.0).astype(BF16)

    pl.semaphore_wait(barrier, PEERS - 1 + 3)

    ring(0, 0).start()
    ring(1, 0).start()
    share(0).start()

    for c in loads:
        c.wait()

    def send_chunk(chunk):
        rows = mm(table(*place(row, chunk)), both[...], 1, 0).astype(BF16)
        sa[pl.ds(chunk * 8, 8)] = rows.reshape(8, 16, D)

        def go(i):
            disp_a(chunk * 8 + i).start()

        loop(jnp.where(chunk == 0, 1, 0), 8, go)

    send_chunk(0)
    rest = mm(table(*place_rest(row)), both[...], 1, 0)
    for i in range(PEERS):
        sb[i] = rest[4 * i : 4 * i + 4].astype(BF16)
    loop(1, PEERS, lambda i: disp_b(i).start())
    loop(1, NX, send_chunk)
    ra[0] = sa[0]
    rb[0] = sb[0]
    for m in range(3):
        w[m, pl.ds(pl.multiple_of(g_me * 128, 128), 128), :] = w_ref[m]
    for chunk in range(NX):
        table_back(chunk, *place(lane, chunk))
    table_back(NX, *place_rest(lane))

    for dist in range(1, 5):
        ring_in(0, dist).wait_recv()
        if dist < 4:
            ring(0, dist).start()
        share(-dist).start()
        if dist < 4:
            ring_in(1, dist).wait_recv()
            if dist < 3:
                ring(1, dist).start()
            share(dist).start()
    for rel in range(-4, 4):
        share_in(rel).wait_recv()

    frow = lax.broadcasted_iota(jnp.int32, (TOK, FF), 0)
    hrow = lax.broadcasted_iota(jnp.int32, (TOK, HALF), 0)

    def expert(chunk, sh):
        x = ra[pl.ds(chunk * 8, 8)].reshape(TOK, D)
        gate = mm(x, w[0], 1, 0)
        up = mm(x, w[1], 1, 0)
        gh = pltpu.roll(mm(x, w[2], 1, 0), TOK - sh, 0)
        logistic = jax.nn.sigmoid(gate)
        swish = gate * logistic
        hidden = swish * up
        grad_up = gh * swish
        grad_gate = gh * up * logistic * (1.0 + gate * (1.0 - logistic))
        keep = (frow & (2 * sh - 1)) < sh
        at = pl.ds(chunk * 128, 128)
        zg = jnp.where(keep, grad_gate, 0.0).astype(BF16)
        zu = jnp.where(keep, grad_up, 0.0).astype(BF16)
        z[at, 0:FF] = zg
        z[at, FF : 2 * FF] = zu
        z[at, 2 * FF : 3 * FF] = jnp.where(keep, 0.0, pltpu.roll(hidden, sh, 0)).astype(BF16)
        return zg, zu

    def back(zg, zu, sh):
        b = mm(zg, w[0], 1, 1) + mm(zu, w[1], 1, 1)
        keep = (hrow & (2 * sh - 1)) < sh
        return jnp.where(keep, b[:, :HALF], pltpu.roll(b[:, HALF:], sh, 0))

    def back_a(chunk, zg, zu):
        ba[pl.ds(chunk * 8, 8)] = back(zg, zu, 8).astype(BF16).reshape(8, 16, HALF)

    def recv_a(chunk):
        loop(jnp.where(chunk == 0, 1, 0), 8, lambda i: disp_a(chunk * 8 + i).wait_recv())

    def early(chunk):
        recv_a(chunk)
        back_a(chunk, *expert(chunk, 8))

    def gather4(src, dst, q):
        rows = jnp.concatenate([src[4 * q + i].astype(F32) for i in range(4)], axis=0)
        dst[PEERS + q] = rows.astype(BF16)

    loop(0, 1, early)
    loop(1, PEERS, lambda i: disp_b(i).wait_recv())
    loop(0, 8, lambda q: gather4(rb, ra, q))
    packed = back(*expert(4, 2), 2)
    for i in range(PEERS):
        bb[i] = packed[4 * i : 4 * i + 4].astype(BF16)
    loop(1, NX - 1, early)

    recv_a(NX - 1)
    loop(1, 8 * (NX - 1), lambda i: ret_a(i).start())
    loop(1, PEERS, lambda i: ret_b(i).start())
    zg, zu = expert(NX - 1, 8)

    def pair(rel):
        return remote(pxs.at[rel], pxr.at[rel], px_s.at[rel], px_r.at[rel], dp=partner)

    def block(j):
        half = j // 2 + 1
        rel = jnp.where(j == 7, 0, jnp.where(j % 2 == 0, NY - half, half))
        y = (my + rel) % NY

        def part(core):
            cols = pl.ds(pl.multiple_of((y * 2 + core) * 128, 128), 128)
            return mm(ra[:, :, cols].reshape(5 * TOK, 128), z[...], 0, 0)

        theirs = part(other)
        for m in range(3):
            pxs[rel, m] = theirs[:, FF * m : FF * (m + 1)].astype(BF16)
        pair(rel).start()
        mine = part(mc)
        for m in range(3):
            own[rel, m] = mine[:, FF * m : FF * (m + 1)]

    loop(0, 8, block)
    back_a(NX - 1, zg, zu)
    loop(8 * (NX - 1), PEERS, lambda i: ret_a(i).start())
    ca[0] = ba[0]
    cb[0] = bb[0]

    def hop(lane, s, m):
        return remote(
            rss.at[lane, s, m], rsr.at[lane, s, m], rs_s.at[lane, s, m], rs_r.at[lane, s, m],
            dp=along(1 - 2 * lane),
        )

    def total(lane, rel, m, s):
        rows = slice(64 * lane, 64 * lane + 64)
        t = own[rel, m, rows, :] + pxr[rel, m, rows, :].astype(F32)
        if s > 0:
            hop(lane, s - 1, m).wait_recv()
            t = t + rsr[lane, s - 1, m].astype(F32)
        return t

    for s in range(7):
        for lane_ in range(2):
            rel = 7 - s if lane_ == 0 else 1 + s
            if s < 3 or (s == 3 and lane_ == 0):
                pair(rel).wait_recv()
            for m in range(3):
                rss[lane_, s, m] = total(lane_, rel, m, s).astype(BF16)
                hop(lane_, s, m).start()
    pair(0).wait_recv()
    for lane_ in range(2):
        for m in range(3):
            wg_ref[m, 64 * lane_ : 64 * lane_ + 64, :] = total(lane_, 0, m, 7)

    loop(1, PEERS, lambda i: ret_b(i).wait_recv())
    loop(0, 8, lambda q: gather4(cb, ca, q))
    loop(1, PEERS, lambda i: ret_a(i).wait_recv())
    allback = ca[...].reshape(5 * TOK, HALF)
    tg_ref[:, 0:HALF] = mm(tl[...], allback, 1, 0).astype(BF16)
    tg_ref[:, HALF:D] = mm(tr[...], allback, 1, 0).astype(BF16)

    def drain(i):
        disp_a(i).wait_send()
        disp_b(i).wait_send()
        ret_a(i).wait_send()
        ret_b(i).wait_send()

    loop(1, PEERS, drain)
    for dist in range(4):
        ring(0, dist).wait_send()
        if dist < 3:
            ring(1, dist).wait_send()
    for rel in range(-4, 4):
        share(rel).wait_send()
    loop(0, 8, lambda k: pair(k).wait_send())
    for lane_ in range(2):
        for m in range(3):
            loop(0, 7, lambda s, lane_=lane_, m=m: hop(lane_, s, m).wait_send())


def on_device(tokens, out_grad, expert_ids, gates, expert_weights):
    vmem = pl.BlockSpec(memory_space=pltpu.VMEM)
    hbm = pl.BlockSpec(memory_space=pl.ANY)
    dma = pltpu.SemaphoreType.DMA
    token_grads, weight_grads = pl.pallas_call(
        kernel,
        out_shape=(
            jax.ShapeDtypeStruct((TOK, D), BF16),
            jax.ShapeDtypeStruct((3, 128, FF), F32),
        ),
        in_specs=[hbm, hbm, vmem, vmem, vmem],
        out_specs=(vmem, vmem),
        scratch_shapes=[
            pltpu.VMEM((2 * TOK, D), BF16),
            pltpu.VMEM((PEERS, 16, D), BF16),
            pltpu.VMEM((PEERS, 4, D), BF16),
            pltpu.VMEM((PEERS + 8, 16, D), BF16),
            pltpu.VMEM((PEERS, 4, D), BF16),
            pltpu.VMEM((3, D, FF), BF16),
            pltpu.VMEM((5 * TOK, 3 * FF), BF16),
            pltpu.VMEM((PEERS, 16, HALF), BF16),
            pltpu.VMEM((PEERS, 4, HALF), BF16),
            pltpu.VMEM((PEERS + 8, 16, HALF), BF16),
            pltpu.VMEM((PEERS, 4, HALF), BF16),
            pltpu.VMEM((NY, 3, 128, FF), F32),
            pltpu.VMEM((NY, 3, 128, FF), BF16),
            pltpu.VMEM((NY, 3, 128, FF), BF16),
            pltpu.VMEM((2, 7, 3, 64, FF), BF16),
            pltpu.VMEM((2, 7, 3, 64, FF), BF16),
            pltpu.VMEM((TOK, 5 * TOK), BF16),
            pltpu.VMEM((TOK, 5 * TOK), BF16),
            dma((2,)),
            dma((PEERS,)), dma((PEERS,)), dma((PEERS,)), dma((PEERS,)),
            dma((PEERS,)), dma((PEERS,)), dma((PEERS,)), dma((PEERS,)),
            dma((2, 4)), dma((2, 4)), dma((8,)), dma((8,)), dma((8,)), dma((8,)),
            dma((2, 7, 3)), dma((2, 7, 3)),
        ],
        compiler_params=pltpu.CompilerParams(
            collective_id=0, has_side_effects=True, vmem_limit_bytes=60 * 1024 * 1024
        ),
        name="routed_backward",
    )(tokens, out_grad, expert_ids, gates, expert_weights[0])
    return token_grads, weight_grads[None]


def solution(mesh):
    spec = P(("dp", "expert"), None)
    return jax.shard_map(
        on_device,
        mesh=mesh,
        in_specs=(spec, spec, spec, spec, P("expert", None, "dp", None)),
        out_specs=(spec, P("expert", None, "dp", None)),
        check_vma=False,
    )
```

time: 325 us -> 126 us (0.39)
  waiting for transfers between devices: 231 us -> 0 us
  Pallas kernels: 0 us -> 120 us
  starting transfers between devices: 37.8 us -> 0 us
  matrix products: 15.9 us -> 0 us
  between operations: 14.4 us -> 0.66 us
  local copies, waits for them, and re-layouts: 14 us -> 4.9 us
  other arithmetic: 8.77 us -> 0 us
    all_to_all x4 -> x0, waiting for transfers between devices: 230 us -> none  [the longest x1 102 us: on_device(): lax.all_to_all(pieces, 'dp', split_axis=1, concat_axis=1, tiled=True)]
    pallas_call x0 -> x1, Pallas kernels: none -> 120 us  [on_device(): pl.pallas_call(kernel, out_shape=(jax.ShapeDtypeStruct((TOK, D), BF16), j...]
    all_to_all x4 -> x0, starting transfers between devices: 37.8 us -> none  [the longest x1 13.6 us: on_device(): lax.all_to_all(sent_rows, 'expert', split_axis=0, concat_axis=0, tiled=True)]
    dot_general x11 -> x0, matrix products: 15.9 us -> none  [the longest x4 7.57 us: inner_rows(): lax.dot_general(first_op, second_op, (((0,), (0,)), ((), ())), preferred_...]
    reshape x6 -> x0, local copies, waits for them, and re-layouts: 11.8 us -> none  [the longest x1 3.35 us: on_device(): sent_grads = sent_grads.reshape(window, SLOTS, model_width)]
    reduce_sum x3 -> x0, other arithmetic: 5.35 us -> none  [the longest x1 3.96 us: on_device(): weight_grads = jnp.sum(received.astype(jnp.float32), axis=1)]
  transfers between devices with their start and end apart: 5 -> 0, of which waited for: 4 -> 0; matrix products, arithmetic and copies ran while one was open for 8% -> 0% of each run, Pallas kernels for 0% -> 0%
where the time goes in v1:
time: 126 us
  Pallas kernels  120 us (95%)
  local copies, waits for them, and re-layouts  4.9 us (4%)
    pallas_call x1, Pallas kernels, on_device(): pl.pallas_call(kernel, out_shape=(jax.ShapeDtypeStruct((TOK, D), BF16), j...  120 us
    unnamed x8, local copies, waits for them, and re-layouts  4.9 us

profile of v1, /device:TPU:6, one launch (start us, length us, event | category | flops | bytes accessed | tf_op | source)
XLA Modules:
  0.0 125.8 jit_solution(9424571682965390894)
XLA Ops:
  0.6 0.0 copy-start.1
  0.6 1.4 %copy.8.gates_ref = bf16[128,8]{1,0:T(8,128)(2,1)} copy(bf16[128,8]{0,1:T(8,128)(2,1)} %param.8) | data formatting | bytes 4096 | tf_op args[3]
  2.0 0.0 copy-done.1
  2.0 0.7 copy.7.ids_ref
  2.8 120.2 %routed_backward.1 = (bf16[128,2048]{1,0:T(8,128)(2,1)}, f32[3,128,384]{2,1,0:T(8,128)}) custom-call(bf16[128,2048]{1,0:T(8,128)(2,1)} %tok_ref.1, bf16[128,2048]{1,0:T(8,128)(2,1)} %og_ref.1, s32[128,8]{1,0:T(8,128)} %copy.7.ids_ref, bf16[128,8]{1,0:T(8,128)(2,1)} %copy.8.gates_ref, bf16[3,128,384]{2,1,0:T(8,128)(2,1)} %bitcast.3), custom_call_target="tpu_custom_call" | custom-call | tf_op jit(solution)/shard_map/routed_backward/pallas_call | solution.py:324
  123.0 0.0 copy-start
  123.0 1.9 %copy.11 = bf16[128,2048]{1,0:T(8,128)(2,1)} copy(bf16[128,2048]{1,0:T(8,128)(2,1)} %get-tuple-element.8) | data formatting | bytes 1048576
  125.0 0.0 copy-done
  125.0 0.8 copy.12
Async XLA Ops:
  0.6 1.4 %copy-start.1 = (s32[128,8]{0,1:T(8,128)S(1)}, s32[128,8]{0,1:T(8,128)}, u32[]{:S(2)}) copy-start(s32[128,8]{0,1:T(8,128)} %param.7) | copy-start | bytes 12292
  123.0 2.0 %copy-start = (f32[3,128,384]{2,1,0:T(8,128)S(1)}, f32[3,128,384]{2,1,0:T(8,128)}, u32[]{:S(2)}) copy-start(f32[3,128,384]{2,1,0:T(8,128)} %get-tuple-element.5) | copy-start | bytes 1769476

commit v2 on v1

--- a/solution.py
+++ b/solution.py
@@ -20,7 +20,7 @@
 def kernel(
     tok_ref, og_ref, ids_ref, gates_ref, w_ref,
     tg_ref, wg_ref,
-    both, sa, sb, ra, rb, w, z, ba, bb, ca, cb, own, pxs, pxr, rss, rsr, tl, tr,
+    both, sa, sb, ra, rb, w, z, ba, bb, ca, cb, own, pxs, pxr, rss, rsr, tl, tr, acc,
     load_sem, sa_s, sa_r, sb_s, sb_r, ba_s, ba_r, bb_s, bb_r,
     ring_s, ring_r, par_s, par_r, px_s, px_r, rs_s, rs_r,
 ):
@@ -66,29 +66,29 @@
     def ring(lane, dist):
         step = 1 - 2 * lane
         g = along(-step * dist)
-        src = w_ref if dist == 0 else shard(g)
-        return remote(src, shard(g), ring_s.at[lane, dist], ring_r.at[lane, dist], dp=along(step))
+        return remote(shard(g), shard(g), ring_s.at[lane, dist], ring_r.at[lane, dist], dp=along(step))
 
     def ring_in(lane, dist):
         step = 1 - 2 * lane
         g = along(-step * dist)
         return remote(
-            w_ref, shard(g), ring_s.at[lane, dist - 1], ring_r.at[lane, dist - 1], dp=along(step)
+            shard(g), shard(g), ring_s.at[lane, dist - 1], ring_r.at[lane, dist - 1], dp=along(step)
         )
 
     def share(rel):
         g = along(rel)
-        src = w_ref if rel == 0 else shard(g)
-        return remote(src, shard(g), par_s.at[rel + 4], par_r.at[rel + 4], dp=partner)
+        return remote(shard(g), shard(g), par_s.at[rel + 4], par_r.at[rel + 4], dp=partner)
 
     def share_in(rel):
         g = ((my + NY + rel) % NY) * 2 + other
-        return remote(w_ref, shard(g), par_s.at[rel + 4], par_r.at[rel + 4], dp=partner)
+        return remote(shard(g), shard(g), par_s.at[rel + 4], par_r.at[rel + 4], dp=partner)
 
     loads = [
         pltpu.make_async_copy(tok_ref, both.at[pl.ds(0, TOK)], load_sem.at[0]),
         pltpu.make_async_copy(og_ref, both.at[pl.ds(TOK, TOK)], load_sem.at[1]),
     ]
+    load_w = pltpu.make_async_copy(w_ref, shard(g_me), load_sem.at[2])
+    load_w.start()
     for c in loads:
         c.start()
 
@@ -105,14 +105,14 @@
     row = lax.broadcasted_iota(jnp.int32, (TOK, 128), 0)
     ids = ids_ref[...]
     gates = gates_ref[...].astype(F32)
-    named = jnp.zeros((TOK, 128), F32)
-    gate_of = jnp.zeros((TOK, 128), F32)
+    named = jnp.zeros((128, TOK), F32)
+    gate_of = jnp.zeros((128, TOK), F32)
     for k in range(8):
-        hit = ids[:, k : k + 1] == lane
+        hit = ids[k : k + 1, :] == row
         named = named + jnp.where(hit, 1.0, 0.0)
-        gate_of = gate_of + jnp.where(hit, gates[:, k : k + 1], 0.0)
-    earlier = jnp.where(lane < row, 1.0, 0.0).astype(BF16)
-    before = mm(earlier, named.astype(BF16), 1, 0)
+        gate_of = gate_of + jnp.where(hit, gates[k : k + 1, :], 0.0)
+    earlier = jnp.where(row < lane, 1.0, 0.0).astype(BF16)
+    before = mm(named.astype(BF16), earlier, 1, 0)
     slots = jnp.where(named > 0.5, before, -1.0).astype(BF16)
     gate_of = gate_of.astype(BF16)
 
@@ -127,46 +127,42 @@
 
     def table(dest, wanted, upper):
         pick = jnp.where(lane == dest, 1.0, 0.0).astype(BF16)
-        hit = mm(pick, slots, 1, 1) == wanted
-        gate = mm(pick, gate_of, 1, 1)
+        hit = mm(pick, slots, 1, 0) == wanted
+        gate = mm(pick, gate_of, 1, 0)
         first = jnp.where(hit & jnp.logical_not(upper), 1.0, 0.0).astype(BF16)
         second = jnp.where(hit & upper, gate, 0.0).astype(BF16)
         return jnp.concatenate([first, second], axis=1)
 
     def table_back(chunk, dest, wanted, upper):
         pick = jnp.where(row == dest, 1.0, 0.0).astype(BF16)
-        hit = mm(slots, pick, 1, 0) == wanted
+        hit = mm(slots, pick, 0, 0) == wanted
         tl[:, pl.ds(128 * chunk, 128)] = jnp.where(hit & jnp.logical_not(upper), 1.0, 0.0).astype(BF16)
         tr[:, pl.ds(128 * chunk, 128)] = jnp.where(hit & upper, 1.0, 0.0).astype(BF16)
 
+    def fill_chunk(chunk):
+        rows = mm(table(*place(row, chunk)), both[...], 1, 0).astype(BF16)
+        sa[pl.ds(chunk * 8, 8)] = rows.reshape(8, 16, D)
+
+    def send_chunk(chunk):
+        loop(jnp.where(chunk == 0, 1, 0), 8, lambda i: disp_a(chunk * 8 + i).start())
+
+    for c in loads:
+        c.wait()
+    fill_chunk(0)
+    load_w.wait()
     pl.semaphore_wait(barrier, PEERS - 1 + 3)
 
+    send_chunk(0)
     ring(0, 0).start()
     ring(1, 0).start()
     share(0).start()
-
-    for c in loads:
-        c.wait()
-
-    def send_chunk(chunk):
-        rows = mm(table(*place(row, chunk)), both[...], 1, 0).astype(BF16)
-        sa[pl.ds(chunk * 8, 8)] = rows.reshape(8, 16, D)
-
-        def go(i):
-            disp_a(chunk * 8 + i).start()
-
-        loop(jnp.where(chunk == 0, 1, 0), 8, go)
-
-    send_chunk(0)
     rest = mm(table(*place_rest(row)), both[...], 1, 0)
     for i in range(PEERS):
         sb[i] = rest[4 * i : 4 * i + 4].astype(BF16)
     loop(1, PEERS, lambda i: disp_b(i).start())
-    loop(1, NX, send_chunk)
+    loop(1, NX, lambda chunk: (fill_chunk(chunk), send_chunk(chunk)))
     ra[0] = sa[0]
     rb[0] = sb[0]
-    for m in range(3):
-        w[m, pl.ds(pl.multiple_of(g_me * 128, 128), 128), :] = w_ref[m]
     for chunk in range(NX):
         table_back(chunk, *place(lane, chunk))
     table_back(NX, *place_rest(lane))
@@ -241,9 +237,7 @@
     def pair(rel):
         return remote(pxs.at[rel], pxr.at[rel], px_s.at[rel], px_r.at[rel], dp=partner)
 
-    def block(j):
-        half = j // 2 + 1
-        rel = jnp.where(j == 7, 0, jnp.where(j % 2 == 0, NY - half, half))
+    def block(rel):
         y = (my + rel) % NY
 
         def part(core):
@@ -258,45 +252,66 @@
         for m in range(3):
             own[rel, m] = mine[:, FF * m : FF * (m + 1)]
 
-    loop(0, 8, block)
+    def blocks(p):
+        loop(0, 2, lambda j: block(jnp.where(j == 0, 7 - p, (1 + p) % 4)))
+
+    def hop(lane, s, k):
+        return remote(
+            rss.at[lane, s, k], rsr.at[lane, s, k], rs_s.at[lane, s, k], rs_r.at[lane, s, k],
+            dp=along(1 - 2 * lane),
+        )
+
+    def total(lane, rel, s, k):
+        rows = slice(64 * lane + 32 * (k % 2), 64 * lane + 32 * (k % 2) + 32)
+        t = own[rel, k // 2, rows, :] + pxr[rel, k // 2, rows, :].astype(F32)
+        if s > 0:
+            hop(lane, s - 1, k).wait_recv()
+            t = t + rsr[lane, s - 1, k].astype(F32)
+        return t
+
+    def hops(s):
+        for lane_ in range(2):
+            rel = 7 - s if lane_ == 0 else 1 + s
+            if s < 3 or (s == 3 and lane_ == 0):
+                pair(rel).wait_recv()
+            for k in range(6):
+                rss[lane_, s, k] = total(lane_, rel, s, k).astype(BF16)
+                hop(lane_, s, k).start()
+
+    def combine(lo, n):
+        part = ca[8 * lo : 8 * (lo + n)].reshape(n * TOK, HALF)
+        cols = slice(TOK * lo, TOK * (lo + n))
+        return mm(tl[:, cols], part, 1, 0), mm(tr[:, cols], part, 1, 0)
+
+    blocks(0)
+    blocks(1)
+    hops(0)
+    blocks(2)
+    hops(1)
+    blocks(3)
+    hops(2)
     back_a(NX - 1, zg, zu)
     loop(8 * (NX - 1), PEERS, lambda i: ret_a(i).start())
     ca[0] = ba[0]
     cb[0] = bb[0]
-
-    def hop(lane, s, m):
-        return remote(
-            rss.at[lane, s, m], rsr.at[lane, s, m], rs_s.at[lane, s, m], rs_r.at[lane, s, m],
-            dp=along(1 - 2 * lane),
-        )
-
-    def total(lane, rel, m, s):
-        rows = slice(64 * lane, 64 * lane + 64)
-        t = own[rel, m, rows, :] + pxr[rel, m, rows, :].astype(F32)
-        if s > 0:
-            hop(lane, s - 1, m).wait_recv()
-            t = t + rsr[lane, s - 1, m].astype(F32)
-        return t
-
-    for s in range(7):
-        for lane_ in range(2):
-            rel = 7 - s if lane_ == 0 else 1 + s
-            if s < 3 or (s == 3 and lane_ == 0):
-                pair(rel).wait_recv()
-            for m in range(3):
-                rss[lane_, s, m] = total(lane_, rel, m, s).astype(BF16)
-                hop(lane_, s, m).start()
+    for s in range(3, 7):
+        hops(s)
+    loop(1, 16, lambda i: ret_a(i).wait_recv())
+    lo, hi = combine(0, 2)
+    acc[:, 0:HALF] = lo
+    acc[:, HALF:D] = hi
     pair(0).wait_recv()
     for lane_ in range(2):
-        for m in range(3):
-            wg_ref[m, 64 * lane_ : 64 * lane_ + 64, :] = total(lane_, 0, m, 7)
+        for k in range(6):
+            at = 64 * lane_ + 32 * (k % 2)
+            wg_ref[k // 2, at : at + 32, :] = total(lane_, 0, 7, k)
 
     loop(1, PEERS, lambda i: ret_b(i).wait_recv())
     loop(0, 8, lambda q: gather4(cb, ca, q))
-    loop(1, PEERS, lambda i: ret_a(i).wait_recv())
-    allback = ca[...].reshape(5 * TOK, HALF)
-    tg_ref[:, 0:HALF] = mm(tl[...], allback, 1, 0).astype(BF16)
-    tg_ref[:, HALF:D] = mm(tr[...], allback, 1, 0).astype(BF16)
+    loop(16, PEERS, lambda i: ret_a(i).wait_recv())
+    lo, hi = combine(2, 3)
+    tg_ref[:, 0:HALF] = (acc[:, 0:HALF] + lo).astype(BF16)
+    tg_ref[:, HALF:D] = (acc[:, HALF:D] + hi).astype(BF16)
 
     def drain(i):
         disp_a(i).wait_send()
@@ -313,8 +328,22 @@
         share(rel).wait_send()
     loop(0, 8, lambda k: pair(k).wait_send())
     for lane_ in range(2):
-        for m in range(3):
-            loop(0, 7, lambda s, lane_=lane_, m=m: hop(lane_, s, m).wait_send())
+        for k in range(6):
+            loop(0, 7, lambda s, lane_=lane_, k=k: hop(lane_, s, k).wait_send())
+
+
+def hand_over(a_ref, b_ref, c_ref, d_ref, a_buf, b_buf, in_sem, out_sem):
+    pieces = [(a_ref.at[pl.ds(32 * i, 32)], a_buf.at[pl.ds(32 * i, 32)], c_ref.at[pl.ds(32 * i, 32)]) for i in range(4)]
+    pieces += [(b_ref.at[i], b_buf.at[i], d_ref.at[i]) for i in range(3)]
+    ins = [pltpu.make_async_copy(p[0], p[1], in_sem.at[i]) for i, p in enumerate(pieces)]
+    outs = [pltpu.make_async_copy(p[1], p[2], out_sem.at[i]) for i, p in enumerate(pieces)]
+    for c in ins:
+        c.start()
+    for i in range(7):
+        ins[i].wait()
+        outs[i].start()
+    for c in outs:
+        c.wait()
 
 
 def on_device(tokens, out_grad, expert_ids, gates, expert_weights):
@@ -327,7 +356,7 @@
             jax.ShapeDtypeStruct((TOK, D), BF16),
             jax.ShapeDtypeStruct((3, 128, FF), F32),
         ),
-        in_specs=[hbm, hbm, vmem, vmem, vmem],
+        in_specs=[hbm, hbm, vmem, vmem, hbm],
         out_specs=(vmem, vmem),
         scratch_shapes=[
             pltpu.VMEM((2 * TOK, D), BF16),
@@ -344,21 +373,38 @@
             pltpu.VMEM((NY, 3, 128, FF), F32),
             pltpu.VMEM((NY, 3, 128, FF), BF16),
             pltpu.VMEM((NY, 3, 128, FF), BF16),
-            pltpu.VMEM((2, 7, 3, 64, FF), BF16),
-            pltpu.VMEM((2, 7, 3, 64, FF), BF16),
+            pltpu.VMEM((2, 7, 6, 32, FF), BF16),
+            pltpu.VMEM((2, 7, 6, 32, FF), BF16),
             pltpu.VMEM((TOK, 5 * TOK), BF16),
             pltpu.VMEM((TOK, 5 * TOK), BF16),
-            dma((2,)),
+            pltpu.VMEM((TOK, D), F32),
+            dma((3,)),
             dma((PEERS,)), dma((PEERS,)), dma((PEERS,)), dma((PEERS,)),
             dma((PEERS,)), dma((PEERS,)), dma((PEERS,)), dma((PEERS,)),
             dma((2, 4)), dma((2, 4)), dma((8,)), dma((8,)), dma((8,)), dma((8,)),
-            dma((2, 7, 3)), dma((2, 7, 3)),
+            dma((2, 7, 6)), dma((2, 7, 6)),
         ],
         compiler_params=pltpu.CompilerParams(
             collective_id=0, has_side_effects=True, vmem_limit_bytes=60 * 1024 * 1024
         ),
         name="routed_backward",
-    )(tokens, out_grad, expert_ids, gates, expert_weights[0])
+    )(tokens, out_grad, expert_ids.T, gates.T, expert_weights[0])
+    token_grads, weight_grads = pl.pallas_call(
+        hand_over,
+        out_shape=(
+            jax.ShapeDtypeStruct((TOK, D), BF16),
+            jax.ShapeDtypeStruct((3, 128, FF), F32),
+        ),
+        in_specs=[hbm, hbm],
+        out_specs=(hbm, hbm),
+        scratch_shapes=[
+            pltpu.VMEM((TOK, D), BF16),
+            pltpu.VMEM((3, 128, FF), F32),
+            dma((7,)), dma((7,)),
+        ],
+        compiler_params=pltpu.CompilerParams(vmem_limit_bytes=60 * 1024 * 1024),
+        name="hand_over",
+    )(token_grads, weight_grads)
     return token_grads, weight_grads[None]
 
 

time: 126 us -> 119 us (0.944)
  local copies, waits for them, and re-layouts: 4.9 us -> 0 us
  Pallas kernels: 120 us -> 118 us
    unnamed x8 -> x0, local copies, waits for them, and re-layouts: 4.9 us -> none
    pallas_call x1, Pallas kernels: 120 us -> 116 us  [on_device(): pl.pallas_call(kernel, out_shape=(jax.ShapeDtypeStruct((TOK, D), BF16), j...]
    pallas_call x0 -> x1, Pallas kernels: none -> 2.11 us  [on_device(): pl.pallas_call(hand_over, out_shape=(jax.ShapeDtypeStruct((TOK, D), BF16)...]
where the time goes in v2:
time: 119 us; the launch traced here: 118 us
  Pallas kernels  118 us (99%)
    pallas_call x1, Pallas kernels, on_device(): pl.pallas_call(kernel, out_shape=(jax.ShapeDtypeStruct((TOK, D), BF16), j...  116 us

profile of v2, /device:TPU:6, one launch (start us, length us, event | category | flops | bytes accessed | tf_op | source)
XLA Modules:
  0.0 118.4 jit_solution(11861195758011142303)
XLA Ops:
  0.6 115.7 %routed_backward.1 = (bf16[128,2048]{1,0:T(8,128)(2,1)}, f32[3,128,384]{2,1,0:T(8,128)}) custom-call(bf16[128,2048]{1,0:T(8,128)(2,1)} %tok_ref.1, bf16[128,2048]{1,0:T(8,128)(2,1)} %og_ref.1, s32[8,128]{1,0:T(8,128)} %bitcast.5, bf16[8,128]{1,0:T(8,128)(2,1)} %bitcast.6, bf16[3,128,384]{2,1,0:T(8,128)(2,1)} %bitcast.4), custom_call_target="tpu_custom_call" | custom-call | tf_op jit(solution)/shard_map/routed_backward/pallas_call | solution.py:353
  116.3 2.1 %hand_over.1 = (bf16[128,2048]{1,0:T(8,128)(2,1)}, f32[3,128,384]{2,1,0:T(8,128)}) custom-call(bf16[128,2048]{1,0:T(8,128)(2,1)} %get-tuple-element.6.a_ref, f32[3,128,384]{2,1,0:T(8,128)} %get-tuple-element.7.b_ref), custom_call_target="tpu_custom_call" | custom-call | tf_op jit(solution)/shard_map/hand_over/pallas_call | solution.py:392

commit v3 on v2

--- a/solution.py
+++ b/solution.py
@@ -20,7 +20,7 @@
 def kernel(
     tok_ref, og_ref, ids_ref, gates_ref, w_ref,
     tg_ref, wg_ref,
-    both, sa, sb, ra, rb, w, z, ba, bb, ca, cb, own, pxs, pxr, rss, rsr, tl, tr, acc,
+    both, sa, sb, ra, rb, w, z, ba, bb, ca, cb, own, pxs, pxr, rss, rsr, tl, tr, acc, pre, tg, wg,
     load_sem, sa_s, sa_r, sb_s, sb_r, ba_s, ba_r, bb_s, bb_r,
     ring_s, ring_r, par_s, par_r, px_s, px_r, rs_s, rs_r,
 ):
@@ -229,28 +229,43 @@
         bb[i] = packed[4 * i : 4 * i + 4].astype(BF16)
     loop(1, NX - 1, early)
 
+    def columns(rel, core):
+        y = (my + rel) % NY
+        return pl.ds(pl.multiple_of((y * 2 + core) * 128, 128), 128)
+
+    def ahead_block(rel):
+        def part(core):
+            cols = columns(rel, core)
+            return mm(ra[0:24, :, cols].reshape(3 * TOK, 128), z[0 : 3 * TOK, :], 0, 0) + mm(
+                ra[32:40, :, cols].reshape(TOK, 128), z[4 * TOK : 5 * TOK, :], 0, 0
+            )
+
+        pre[rel] = part(other)
+        mine = part(mc)
+        for m in range(3):
+            own[rel, m] = mine[:, FF * m : FF * (m + 1)]
+
+    loop(0, 8, ahead_block)
+
     recv_a(NX - 1)
-    loop(1, 8 * (NX - 1), lambda i: ret_a(i).start())
-    loop(1, PEERS, lambda i: ret_b(i).start())
+    loop(1, 8, lambda i: ret_a(i).start())
     zg, zu = expert(NX - 1, 8)
 
     def pair(rel):
         return remote(pxs.at[rel], pxr.at[rel], px_s.at[rel], px_r.at[rel], dp=partner)
 
     def block(rel):
-        y = (my + rel) % NY
-
         def part(core):
-            cols = pl.ds(pl.multiple_of((y * 2 + core) * 128, 128), 128)
-            return mm(ra[:, :, cols].reshape(5 * TOK, 128), z[...], 0, 0)
-
-        theirs = part(other)
+            x = ra[24:32, :, columns(rel, core)].reshape(TOK, 128)
+            return mm(x, z[3 * TOK : 4 * TOK, :], 0, 0)
+
+        theirs = pre[rel] + part(other)
         for m in range(3):
             pxs[rel, m] = theirs[:, FF * m : FF * (m + 1)].astype(BF16)
         pair(rel).start()
         mine = part(mc)
         for m in range(3):
-            own[rel, m] = mine[:, FF * m : FF * (m + 1)]
+            own[rel, m] += mine[:, FF * m : FF * (m + 1)]
 
     def blocks(p):
         loop(0, 2, lambda j: block(jnp.where(j == 0, 7 - p, (1 + p) % 4)))
@@ -270,12 +285,13 @@
         return t
 
     def hops(s):
+        rels = (7 - s, 1 + s)
         for lane_ in range(2):
-            rel = 7 - s if lane_ == 0 else 1 + s
             if s < 3 or (s == 3 and lane_ == 0):
-                pair(rel).wait_recv()
-            for k in range(6):
-                rss[lane_, s, k] = total(lane_, rel, s, k).astype(BF16)
+                pair(rels[lane_]).wait_recv()
+        for k in range(6):
+            for lane_ in range(2):
+                rss[lane_, s, k] = total(lane_, rels[lane_], s, k).astype(BF16)
                 hop(lane_, s, k).start()
 
     def combine(lo, n):
@@ -286,6 +302,8 @@
     blocks(0)
     blocks(1)
     hops(0)
+    loop(8, 8 * (NX - 1), lambda i: ret_a(i).start())
+    loop(1, PEERS, lambda i: ret_b(i).start())
     blocks(2)
     hops(1)
     blocks(3)
@@ -304,14 +322,20 @@
     for lane_ in range(2):
         for k in range(6):
             at = 64 * lane_ + 32 * (k % 2)
-            wg_ref[k // 2, at : at + 32, :] = total(lane_, 0, 7, k)
+            wg[k // 2, at : at + 32, :] = total(lane_, 0, 7, k)
+    out_w = pltpu.make_async_copy(wg, wg_ref, load_sem.at[3])
+    out_w.start()
 
     loop(1, PEERS, lambda i: ret_b(i).wait_recv())
     loop(0, 8, lambda q: gather4(cb, ca, q))
     loop(16, PEERS, lambda i: ret_a(i).wait_recv())
     lo, hi = combine(2, 3)
-    tg_ref[:, 0:HALF] = (acc[:, 0:HALF] + lo).astype(BF16)
-    tg_ref[:, HALF:D] = (acc[:, HALF:D] + hi).astype(BF16)
+    outs = []
+    for i, part in enumerate((lo, hi)):
+        cols = pl.ds(HALF * i, HALF)
+        tg[:, cols] = (acc[:, cols] + part).astype(BF16)
+        outs.append(pltpu.make_async_copy(tg.at[:, cols], tg_ref.at[:, cols], load_sem.at[4 + i]))
+        outs[i].start()
 
     def drain(i):
         disp_a(i).wait_send()
@@ -320,6 +344,8 @@
         ret_b(i).wait_send()
 
     loop(1, PEERS, drain)
+    for c in [out_w] + outs:
+        c.wait()
     for dist in range(4):
         ring(0, dist).wait_send()
         if dist < 3:
@@ -357,7 +383,7 @@
             jax.ShapeDtypeStruct((3, 128, FF), F32),
         ),
         in_specs=[hbm, hbm, vmem, vmem, hbm],
-        out_specs=(vmem, vmem),
+        out_specs=(hbm, hbm),
         scratch_shapes=[
             pltpu.VMEM((2 * TOK, D), BF16),
             pltpu.VMEM((PEERS, 16, D), BF16),
@@ -378,7 +404,10 @@
             pltpu.VMEM((TOK, 5 * TOK), BF16),
             pltpu.VMEM((TOK, 5 * TOK), BF16),
             pltpu.VMEM((TOK, D), F32),
-            dma((3,)),
+            pltpu.VMEM((NY, TOK, 3 * FF), F32),
+            pltpu.VMEM((TOK, D), BF16),
+            pltpu.VMEM((3, 128, FF), F32),
+            dma((6,)),
             dma((PEERS,)), dma((PEERS,)), dma((PEERS,)), dma((PEERS,)),
             dma((PEERS,)), dma((PEERS,)), dma((PEERS,)), dma((PEERS,)),
             dma((2, 4)), dma((2, 4)), dma((8,)), dma((8,)), dma((8,)), dma((8,)),

time: 119 us -> 114 us (0.958)
  Pallas kernels: 118 us -> 113 us
    pallas_call x1, Pallas kernels: 116 us -> 111 us  [on_device(): pl.pallas_call(kernel, out_shape=(jax.ShapeDtypeStruct((TOK, D), BF16), j...]
where the time goes in v3:
time: 114 us; the launch traced here: 113 us
  Pallas kernels  113 us (99%)
    pallas_call x1, Pallas kernels, on_device(): pl.pallas_call(kernel, out_shape=(jax.ShapeDtypeStruct((TOK, D), BF16), j...  111 us

profile of v3, /device:TPU:6, one launch (start us, length us, event | category | flops | bytes accessed | tf_op | source)
XLA Modules:
  0.0 113.3 jit_solution(5498070642228860951)
XLA Ops:
  0.6 110.6 %routed_backward.1 = (bf16[128,2048]{1,0:T(8,128)(2,1)}, f32[3,128,384]{2,1,0:T(8,128)}) custom-call(bf16[128,2048]{1,0:T(8,128)(2,1)} %tok_ref.1, bf16[128,2048]{1,0:T(8,128)(2,1)} %og_ref.1, s32[8,128]{1,0:T(8,128)} %bitcast.5, bf16[8,128]{1,0:T(8,128)(2,1)} %bitcast.6, bf16[3,128,384]{2,1,0:T(8,128)(2,1)} %bitcast.4), custom_call_target="tpu_custom_call" | custom-call | tf_op jit(solution)/shard_map/routed_backward/pallas_call | solution.py:379
  111.2 2.1 %hand_over.1 = (bf16[128,2048]{1,0:T(8,128)(2,1)}, f32[3,128,384]{2,1,0:T(8,128)}) custom-call(bf16[128,2048]{1,0:T(8,128)(2,1)} %get-tuple-element.6.a_ref, f32[3,128,384]{2,1,0:T(8,128)} %get-tuple-element.7.b_ref), custom_call_target="tpu_custom_call" | custom-call | tf_op jit(solution)/shard_map/hand_over/pallas_call | solution.py:421

commit v4 on v3

--- a/solution.py
+++ b/solution.py
@@ -11,6 +11,10 @@
 TOK, D, FF = 128, 2048, 384
 HALF = D // 2
 F32, BF16 = jnp.float32, jnp.bfloat16
+FARTHEST = sorted(
+    ((dx, dz) for dx in range(NX) for dz in range(NZ) if dx or dz),
+    key=lambda o: -(min(o[0], NX - o[0]) + min(o[1], NZ - o[1])),
+)
 
 
 def mm(a, b, ca, cb):
@@ -20,25 +24,25 @@
 def kernel(
     tok_ref, og_ref, ids_ref, gates_ref, w_ref,
     tg_ref, wg_ref,
-    both, sa, sb, ra, rb, w, z, ba, bb, ca, cb, own, pxs, pxr, rss, rsr, tl, tr, acc, pre, tg, wg,
+    both, sa, sb, ra, rb, w, z, ba, bb, ca, cb, own, pxs, pxr, rss, rsr, tl, tr, acc, pre, tg, wg, ids_buf, gates_buf,
     load_sem, sa_s, sa_r, sb_s, sb_r, ba_s, ba_r, bb_s, bb_r,
     ring_s, ring_r, par_s, par_r, px_s, px_r, rs_s, rs_r,
 ):
     e_me = lax.axis_index("expert")
     g_me = lax.axis_index("dp")
-    mx, mz = e_me // NZ, e_me % NZ
-    my, mc = g_me // 2, g_me % 2
+    mx, mz = lax.div(e_me, NZ), lax.rem(e_me, NZ)
+    my, mc = lax.div(g_me, 2), lax.rem(g_me, 2)
     other = 1 - mc
     partner = my * 2 + other
 
     def ahead(slot):
-        return ((mx + slot // NZ) % NX) * NZ + (mz + slot % NZ) % NZ
+        return lax.rem(mx + lax.div(slot, NZ), NX) * NZ + lax.rem(mz + lax.rem(slot, NZ), NZ)
 
     def behind(slot):
-        return ((mx + NX - slot // NZ) % NX) * NZ + (mz + NZ - slot % NZ) % NZ
+        return lax.rem(mx + NX - lax.div(slot, NZ), NX) * NZ + lax.rem(mz + NZ - lax.rem(slot, NZ), NZ)
 
     def along(step):
-        return ((my + NY + step) % NY) * 2 + mc
+        return lax.rem(my + NY + step, NY) * 2 + mc
 
     def remote(src, dst, ss, rs, **where):
         return pltpu.make_async_remote_copy(
@@ -80,31 +84,38 @@
         return remote(shard(g), shard(g), par_s.at[rel + 4], par_r.at[rel + 4], dp=partner)
 
     def share_in(rel):
-        g = ((my + NY + rel) % NY) * 2 + other
+        g = lax.rem(my + NY + rel, NY) * 2 + other
         return remote(shard(g), shard(g), par_s.at[rel + 4], par_r.at[rel + 4], dp=partner)
 
+    keys = [
+        pltpu.make_async_copy(ids_ref, ids_buf, load_sem.at[6]),
+        pltpu.make_async_copy(gates_ref, gates_buf, load_sem.at[7]),
+    ]
     loads = [
         pltpu.make_async_copy(tok_ref, both.at[pl.ds(0, TOK)], load_sem.at[0]),
         pltpu.make_async_copy(og_ref, both.at[pl.ds(TOK, TOK)], load_sem.at[1]),
     ]
     load_w = pltpu.make_async_copy(w_ref, shard(g_me), load_sem.at[2])
-    load_w.start()
+    for c in keys:
+        c.start()
+
+    barrier = pltpu.get_barrier_semaphore()
+    rows_x = [lax.rem(mx + dx, NX) * NZ for dx in range(NX)]
+    cols_z = [lax.rem(mz + dz, NZ) for dz in range(NZ)]
+    for dx, dz in FARTHEST:
+        pl.semaphore_signal(barrier, inc=1, device_id={"expert": rows_x[dx] + cols_z[dz]}, device_id_type=MESH)
+    for g in (along(1), along(-1), partner):
+        pl.semaphore_signal(barrier, inc=1, device_id={"dp": g}, device_id_type=MESH)
     for c in loads:
         c.start()
-
-    barrier = pltpu.get_barrier_semaphore()
-
-    def greet(slot):
-        pl.semaphore_signal(barrier, inc=1, device_id={"expert": ahead(slot)}, device_id_type=MESH)
-
-    loop(1, PEERS, greet)
-    for g in (along(1), along(-1), partner):
-        pl.semaphore_signal(barrier, inc=1, device_id={"dp": g}, device_id_type=MESH)
+    load_w.start()
 
     lane = lax.broadcasted_iota(jnp.int32, (TOK, 128), 1)
     row = lax.broadcasted_iota(jnp.int32, (TOK, 128), 0)
-    ids = ids_ref[...]
-    gates = gates_ref[...].astype(F32)
+    for c in keys:
+        c.wait()
+    ids = ids_buf[...]
+    gates = gates_buf[...].astype(F32)
     named = jnp.zeros((128, TOK), F32)
     gate_of = jnp.zeros((128, TOK), F32)
     for k in range(8):
@@ -230,7 +241,7 @@
     loop(1, NX - 1, early)
 
     def columns(rel, core):
-        y = (my + rel) % NY
+        y = lax.rem(my + rel, NY)
         return pl.ds(pl.multiple_of((y * 2 + core) * 128, 128), 128)
 
     def ahead_block(rel):
@@ -300,9 +311,10 @@
         return mm(tl[:, cols], part, 1, 0), mm(tr[:, cols], part, 1, 0)
 
     blocks(0)
+    loop(8, 16, lambda i: ret_a(i).start())
     blocks(1)
+    loop(16, 8 * (NX - 1), lambda i: ret_a(i).start())
     hops(0)
-    loop(8, 8 * (NX - 1), lambda i: ret_a(i).start())
     loop(1, PEERS, lambda i: ret_b(i).start())
     blocks(2)
     hops(1)
@@ -373,7 +385,6 @@
 
 
 def on_device(tokens, out_grad, expert_ids, gates, expert_weights):
-    vmem = pl.BlockSpec(memory_space=pltpu.VMEM)
     hbm = pl.BlockSpec(memory_space=pl.ANY)
     dma = pltpu.SemaphoreType.DMA
     token_grads, weight_grads = pl.pallas_call(
@@ -382,7 +393,7 @@
             jax.ShapeDtypeStruct((TOK, D), BF16),
             jax.ShapeDtypeStruct((3, 128, FF), F32),
         ),
-        in_specs=[hbm, hbm, vmem, vmem, hbm],
+        in_specs=[hbm, hbm, hbm, hbm, hbm],
         out_specs=(hbm, hbm),
         scratch_shapes=[
             pltpu.VMEM((2 * TOK, D), BF16),
@@ -407,7 +418,9 @@
             pltpu.VMEM((NY, TOK, 3 * FF), F32),
             pltpu.VMEM((TOK, D), BF16),
             pltpu.VMEM((3, 128, FF), F32),
-            dma((6,)),
+            pltpu.VMEM((8, TOK), jnp.int32),
+            pltpu.VMEM((8, TOK), BF16),
+            dma((8,)),
             dma((PEERS,)), dma((PEERS,)), dma((PEERS,)), dma((PEERS,)),
             dma((PEERS,)), dma((PEERS,)), dma((PEERS,)), dma((PEERS,)),
             dma((2, 4)), dma((2, 4)), dma((8,)), dma((8,)), dma((8,)), dma((8,)),

time: 114 us -> 113 us (level)
  no operation moved by 1% of the time
where the time goes in v4:
time: 113 us
  Pallas kernels  112 us (99%)
    pallas_call x1, Pallas kernels, on_device(): pl.pallas_call(kernel, out_shape=(jax.ShapeDtypeStruct((TOK, D), BF16), j...  110 us

profile of v4, /device:TPU:6, one launch (start us, length us, event | category | flops | bytes accessed | tf_op | source)
XLA Modules:
  0.0 112.6 jit_solution(10984541721514284335)
XLA Ops:
  0.6 109.8 %routed_backward.1 = (bf16[128,2048]{1,0:T(8,128)(2,1)}, f32[3,128,384]{2,1,0:T(8,128)}) custom-call(bf16[128,2048]{1,0:T(8,128)(2,1)} %tok_ref.1, bf16[128,2048]{1,0:T(8,128)(2,1)} %og_ref.1, s32[8,128]{1,0:T(8,128)} %bitcast.5, bf16[8,128]{1,0:T(8,128)(2,1)} %bitcast.6, bf16[3,128,384]{2,1,0:T(8,128)(2,1)} %bitcast.4), custom_call_target="tpu_custom_call" | custom-call | tf_op jit(solution)/shard_map/routed_backward/pallas_call | solution.py:390
  110.4 2.1 %hand_over.1 = (bf16[128,2048]{1,0:T(8,128)(2,1)}, f32[3,128,384]{2,1,0:T(8,128)}) custom-call(bf16[128,2048]{1,0:T(8,128)(2,1)} %get-tuple-element.6.a_ref, f32[3,128,384]{2,1,0:T(8,128)} %get-tuple-element.7.b_ref), custom_call_target="tpu_custom_call" | custom-call | tf_op jit(solution)/shard_map/hand_over/pallas_call | solution.py:434

commit v5 on v4

--- a/solution.py
+++ b/solution.py
@@ -24,7 +24,7 @@
 def kernel(
     tok_ref, og_ref, ids_ref, gates_ref, w_ref,
     tg_ref, wg_ref,
-    both, sa, sb, ra, rb, w, z, ba, bb, ca, cb, own, pxs, pxr, rss, rsr, tl, tr, acc, pre, tg, wg, ids_buf, gates_buf,
+    both, sa, sb, ra, rb, w, z, ba, bb, ca, cb, own, pxs, pxr, rss, rsr, tl, tr, acc, pre, ids_buf, gates_buf,
     load_sem, sa_s, sa_r, sb_s, sb_r, ba_s, ba_r, bb_s, bb_r,
     ring_s, ring_r, par_s, par_r, px_s, px_r, rs_s, rs_r,
 ):
@@ -334,20 +334,15 @@
     for lane_ in range(2):
         for k in range(6):
             at = 64 * lane_ + 32 * (k % 2)
-            wg[k // 2, at : at + 32, :] = total(lane_, 0, 7, k)
-    out_w = pltpu.make_async_copy(wg, wg_ref, load_sem.at[3])
-    out_w.start()
+            wg_ref[k // 2, at : at + 32, :] = total(lane_, 0, 7, k)
 
     loop(1, PEERS, lambda i: ret_b(i).wait_recv())
     loop(0, 8, lambda q: gather4(cb, ca, q))
     loop(16, PEERS, lambda i: ret_a(i).wait_recv())
     lo, hi = combine(2, 3)
-    outs = []
     for i, part in enumerate((lo, hi)):
         cols = pl.ds(HALF * i, HALF)
-        tg[:, cols] = (acc[:, cols] + part).astype(BF16)
-        outs.append(pltpu.make_async_copy(tg.at[:, cols], tg_ref.at[:, cols], load_sem.at[4 + i]))
-        outs[i].start()
+        tg_ref[:, cols] = (acc[:, cols] + part).astype(BF16)
 
     def drain(i):
         disp_a(i).wait_send()
@@ -356,8 +351,6 @@
         ret_b(i).wait_send()
 
     loop(1, PEERS, drain)
-    for c in [out_w] + outs:
-        c.wait()
     for dist in range(4):
         ring(0, dist).wait_send()
         if dist < 3:
@@ -370,31 +363,27 @@
             loop(0, 7, lambda s, lane_=lane_, k=k: hop(lane_, s, k).wait_send())
 
 
-def hand_over(a_ref, b_ref, c_ref, d_ref, a_buf, b_buf, in_sem, out_sem):
-    pieces = [(a_ref.at[pl.ds(32 * i, 32)], a_buf.at[pl.ds(32 * i, 32)], c_ref.at[pl.ds(32 * i, 32)]) for i in range(4)]
-    pieces += [(b_ref.at[i], b_buf.at[i], d_ref.at[i]) for i in range(3)]
-    ins = [pltpu.make_async_copy(p[0], p[1], in_sem.at[i]) for i, p in enumerate(pieces)]
-    outs = [pltpu.make_async_copy(p[1], p[2], out_sem.at[i]) for i, p in enumerate(pieces)]
-    for c in ins:
+def hand_over(a_ref, b_ref, c_ref, d_ref, sem):
+    outs = [
+        pltpu.make_async_copy(a_ref.at[pl.ds(32 * i, 32)], c_ref.at[pl.ds(32 * i, 32)], sem.at[i])
+        for i in range(4)
+    ]
+    outs += [pltpu.make_async_copy(b_ref.at[i], d_ref.at[i], sem.at[4 + i]) for i in range(3)]
+    for c in outs:
         c.start()
-    for i in range(7):
-        ins[i].wait()
-        outs[i].start()
     for c in outs:
         c.wait()
 
 
 def on_device(tokens, out_grad, expert_ids, gates, expert_weights):
     hbm = pl.BlockSpec(memory_space=pl.ANY)
+    vmem = pl.BlockSpec(memory_space=pltpu.VMEM)
     dma = pltpu.SemaphoreType.DMA
     token_grads, weight_grads = pl.pallas_call(
         kernel,
-        out_shape=(
-            jax.ShapeDtypeStruct((TOK, D), BF16),
-            jax.ShapeDtypeStruct((3, 128, FF), F32),
-        ),
+        out_shape=(pltpu.VMEM((TOK, D), BF16), pltpu.VMEM((3, 128, FF), F32)),
         in_specs=[hbm, hbm, hbm, hbm, hbm],
-        out_specs=(hbm, hbm),
+        out_specs=(vmem, vmem),
         scratch_shapes=[
             pltpu.VMEM((2 * TOK, D), BF16),
             pltpu.VMEM((PEERS, 16, D), BF16),
@@ -416,8 +405,6 @@
             pltpu.VMEM((TOK, 5 * TOK), BF16),
             pltpu.VMEM((TOK, D), F32),
             pltpu.VMEM((NY, TOK, 3 * FF), F32),
-            pltpu.VMEM((TOK, D), BF16),
-            pltpu.VMEM((3, 128, FF), F32),
             pltpu.VMEM((8, TOK), jnp.int32),
             pltpu.VMEM((8, TOK), BF16),
             dma((8,)),
@@ -437,14 +424,10 @@
             jax.ShapeDtypeStruct((TOK, D), BF16),
             jax.ShapeDtypeStruct((3, 128, FF), F32),
         ),
-        in_specs=[hbm, hbm],
+        in_specs=[vmem, vmem],
         out_specs=(hbm, hbm),
-        scratch_shapes=[
-            pltpu.VMEM((TOK, D), BF16),
-            pltpu.VMEM((3, 128, FF), F32),
-            dma((7,)), dma((7,)),
-        ],
-        compiler_params=pltpu.CompilerParams(vmem_limit_bytes=60 * 1024 * 1024),
+        scratch_shapes=[dma((7,))],
+        compiler_params=pltpu.CompilerParams(vmem_limit_bytes=4 * 1024 * 1024),
         name="hand_over",
     )(token_grads, weight_grads)
     return token_grads, weight_grads[None]

time: 113 us -> 112 us (level)
  Pallas kernels: 112 us -> 110 us
where the time goes in v5:
time: 112 us; the launch traced here: 111 us
  Pallas kernels  110 us (98%)
    pallas_call x1, Pallas kernels, on_device(): pl.pallas_call(kernel, out_shape=(pltpu.VMEM((TOK, D), BF16), pltpu.VMEM(...  109 us

profile of v5, /device:TPU:6, one launch (start us, length us, event | category | flops | bytes accessed | tf_op | source)
XLA Modules:
  0.0 111.1 jit_solution(15539607162048688047)
XLA Ops:
  0.6 109.4 %routed_backward.1 = (bf16[128,2048]{1,0:T(8,128)(2,1)S(1)}, f32[3,128,384]{2,1,0:T(8,128)S(1)}) custom-call(bf16[128,2048]{1,0:T(8,128)(2,1)} %tok_ref.1, bf16[128,2048]{1,0:T(8,128)(2,1)} %og_ref.1, s32[8,128]{1,0:T(8,128)} %bitcast.5, bf16[8,128]{1,0:T(8,128)(2,1)} %bitcast.6, bf16[3,128,384]{2,1,0:T(8,128)(2,1)} %bitcast.4), custom_call_target="tpu_custom_call" | custom-call | tf_op jit(solution)/shard_map/routed_backward/pallas_call | solution.py:382
  110.0 1.0 hand_over.1

commit v6 on v5

--- a/solution.py
+++ b/solution.py
@@ -258,8 +258,9 @@
 
     loop(0, 8, ahead_block)
 
-    recv_a(NX - 1)
+    loop(8 * (NX - 1), 8 * (NX - 1) + 4, lambda i: disp_a(i).wait_recv())
     loop(1, 8, lambda i: ret_a(i).start())
+    loop(8 * (NX - 1) + 4, PEERS, lambda i: disp_a(i).wait_recv())
     zg, zu = expert(NX - 1, 8)
 
     def pair(rel):

time: 112 us -> 112 us (level)
  no operation moved by 1% of the time
where the time goes in v6:
time: 112 us; the launch traced here: 111 us
  Pallas kernels  111 us (99%)
    pallas_call x1, Pallas kernels, on_device(): pl.pallas_call(kernel, out_shape=(pltpu.VMEM((TOK, D), BF16), pltpu.VMEM(...  110 us

profile of v6, /device:TPU:6, one launch (start us, length us, event | category | flops | bytes accessed | tf_op | source)
XLA Modules:
  0.0 111.4 jit_solution(865507918661095510)
XLA Ops:
  0.6 109.7 %routed_backward.1 = (bf16[128,2048]{1,0:T(8,128)(2,1)S(1)}, f32[3,128,384]{2,1,0:T(8,128)S(1)}) custom-call(bf16[128,2048]{1,0:T(8,128)(2,1)} %tok_ref.1, bf16[128,2048]{1,0:T(8,128)(2,1)} %og_ref.1, s32[8,128]{1,0:T(8,128)} %bitcast.5, bf16[8,128]{1,0:T(8,128)(2,1)} %bitcast.6, bf16[3,128,384]{2,1,0:T(8,128)(2,1)} %bitcast.4), custom_call_target="tpu_custom_call" | custom-call | tf_op jit(solution)/shard_map/routed_backward/pallas_call | solution.py:383
  110.4 1.0 hand_over.1
